TPU v7x, 512 devices: a whole 4x4x16 slice. The times are simulated.
512 devices in a mesh: seq: 64 (over x, z), tp: 8 (over y, core).
Axes of the slice: x: 4, y: 4, z: 16, core: 2. Of those that a mesh axis runs over, the one named last changes fastest.
Arguments:
- queries: bfloat16 [4, 1024], P(None, 'tp'), may hold values from -6 to 6
- keys_new: bfloat16 [4, 1024], P(None, 'tp'), may hold values from -32 to 32
- values_new: bfloat16 [4, 1024], P(None, 'tp'), may hold values from -6 to 6
- key_cache: bfloat16 [4, 4096, 1024], P(None, 'seq', 'tp'), may hold values from -32 to 32
- value_cache: bfloat16 [4, 4096, 1024], P(None, 'seq', 'tp'), may hold values from -6 to 6
- buckets: int32 [4, 4096], P(None, 'seq'), may hold values from 0 to 31
- lengths: int32 [4], replicated, may hold values from 1 to 4096, as said below
- bias_table: float32 [32, 16], replicated, may hold values from -3 to 3
- out_proj: bfloat16 [1024, 1024], P('tp'), may hold values from -0.1875 to 0.1875
- decode_in: bfloat16 [4, 1024], replicated, may hold values from -6 to 6
- prefill_in: bfloat16 [32768, 1024], P(('seq', 'tp')), may hold values from -6 to 6
- routes: int32 [32768, 2], P(('seq', 'tp')), may hold values from 0 to 15, all different within a row; in each aligned block of 64 rows (0 to 63, 64 to 127, ...) at most 10 rows name the same one
- gates: float32 [32768, 2], P(('seq', 'tp')), may hold values from 0.2 to 1
- dec_routes: int32 [4, 2], replicated, may hold values from 0 to 15, as said below
- dec_gates: float32 [4, 2], replicated, may hold values from 0.2 to 1
- norm_gain: float32 [1024], replicated, may hold values from 0.1 to 1.9
- w_gate: bfloat16 [1024, 45056], P('tp', 'seq'), may hold values from -0.1875 to 0.1875
- w_up: bfloat16 [1024, 45056], P('tp', 'seq'), may hold values from -0.1875 to 0.1875
- w_down: bfloat16 [45056, 1024], P('seq', 'tp'), may hold values from -0.109375 to 0.109375
Outputs:
- decode_out: bfloat16 [4, 1024], replicated
- prefill_out: bfloat16 [32768, 1024], P(('seq', 'tp'))
Inputs may be any that keep to these rules, and one draw needn't show every extreme that they name: `routes`: in the 64 rows of one device no expert is named by more than 10 rows, a bound that some block reaches. `dec_routes`: the two experts of a decode token differ; some decode token names expert 0 and some names expert 16 - 1. `lengths`: some request has all 4096 positions and some has exactly 1.
All inputs are finite; a program needn't handle non-finite values.
Results may differ from a plain program's by a relative error of at most 0.0075.
Values may be sent and summed in bfloat16 or wider, within the bound.
A program may use at most 64 MiB of HBM per device.

v0:
```python
import math
import jax
import jax.numpy as jnp
from jax import lax
from jax.sharding import PartitionSpec as P

HD = 64
EXPERTS = 16
TOP = 2
CAP = 10


def combined_all(value, axis, join):
    pieces = jax.tree.map(lambda part: lax.all_gather(part, axis), value)
    head = jax.tree.map(lambda part: part[0], pieces)
    tail = jax.tree.map(lambda part: part[1:], pieces)
    so_far, _ = lax.scan(lambda so_far, section: (join(so_far, section), None), head, tail)
    return so_far


def rms_scale(hidden, norm_gain):
    values = hidden.astype(jnp.float32)
    meansq = jnp.mean(values * values, axis=-1, keepdims=True)
    return (values * lax.rsqrt(meansq + 1e-06) * norm_gain).astype(jnp.bfloat16)


def combine_parts(earlier, later):
    max_early, sum_early, acc_early = earlier
    max_late, sum_late, acc_late = later
    joint_max = jnp.maximum(max_early, max_late)
    scale_early = jnp.exp(max_early - joint_max)
    scale_late = jnp.exp(max_late - joint_max)
    joint_sum = sum_early * scale_early + sum_late * scale_late
    joint_acc = acc_early * scale_early[..., None] + acc_late * scale_late[..., None]
    return (joint_max, joint_sum, joint_acc)


def route_slots(route_rows, capacity):
    flat_routes = route_rows.reshape(-1)
    onehot = (flat_routes[:, None] == jnp.arange(EXPERTS, dtype=jnp.int32)[None, :]).astype(
        jnp.int32
    )
    earlier = jnp.cumsum(onehot, axis=0) - onehot
    slot_rank = jnp.sum(earlier * onehot, axis=1)
    return flat_routes * capacity + slot_rank


def pack_rows(normed, route_rows, capacity, shards):
    flat_index = route_slots(route_rows, capacity)
    source = jnp.repeat(normed, TOP, axis=0)
    feature_width = normed.shape[1]
    packed = jnp.zeros((EXPERTS * capacity, feature_width), jnp.bfloat16).at[flat_index].set(source)
    packed = packed.reshape(EXPERTS, capacity, feature_width)
    return (jnp.repeat(packed, shards, axis=0), flat_index)


def expert_block(row_block, weights):
    gate_full, up_full, down_full = weights
    gate_pre = jnp.dot(row_block, gate_full, preferred_element_type=jnp.float32)
    up_pre = jnp.dot(row_block, up_full, preferred_element_type=jnp.float32)
    act = (jax.nn.gelu(gate_pre, approximate=True) * up_pre).astype(jnp.bfloat16)
    return jnp.dot(act, down_full, preferred_element_type=jnp.float32).astype(jnp.bfloat16)


def expert_apply(received, weights):
    peer_count, slot_count, feature_width = received.shape
    partial_value = expert_block(received.reshape(peer_count * slot_count, feature_width), weights)
    return partial_value.reshape(peer_count, slot_count, feature_width)


def unpack_rows(returned, flat_index, shards, residual, gate_rows):
    peer_count, slot_count, feature_width = returned.shape
    summed = returned.astype(jnp.float32).reshape(EXPERTS, shards, slot_count, feature_width)
    summed = jnp.sum(summed, axis=1).reshape(EXPERTS * slot_count, feature_width)
    picked = jnp.take(summed, flat_index, axis=0).reshape(-1, TOP, feature_width)
    combined = residual.astype(jnp.float32) + jnp.sum(gate_rows[..., None] * picked, axis=1)
    return combined.astype(jnp.bfloat16)


def body(
    queries,
    keys_new,
    values_new,
    key_cache,
    value_cache,
    buckets,
    lengths,
    bias_table,
    out_proj,
    decode_in,
    prefill_in,
    routes,
    gates,
    dec_routes,
    dec_gates,
    norm_gain,
    w_gate,
    w_up,
    w_down,
):
    seq_count = lax.axis_size("seq")
    seq_index = lax.axis_index("seq")
    tp_index = lax.axis_index("tp")
    shards = seq_count // EXPERTS
    weights = (
        lax.all_gather(w_gate, "tp", axis=0, tiled=True),
        lax.all_gather(w_up, "tp", axis=0, tiled=True),
        lax.all_gather(w_down, "tp", axis=1, tiled=True),
    )
    normed_pre = rms_scale(prefill_in, norm_gain)
    request_count, heads_width = queries.shape
    heads_here = heads_width // HD
    ctx_local = key_cache.shape[1]
    score_scale = 1.0 / math.sqrt(HD)
    query_rows = queries.reshape(request_count, heads_here, HD)
    key_rows = key_cache.reshape(request_count, ctx_local, heads_here, HD)
    value_rows = value_cache.reshape(request_count, ctx_local, heads_here, HD).astype(jnp.float32)
    bias_here = lax.dynamic_slice_in_dim(bias_table, tp_index * heads_here, heads_here, 1)
    bucket_hot = (
        buckets[..., None] == jnp.arange(bias_table.shape[0], dtype=jnp.int32)[None, None, :]
    ).astype(jnp.float32)
    bias_rows = jnp.einsum("rcn,nh->rhc", bucket_hot, bias_here, precision=lax.Precision.HIGHEST)
    cache_scores = (
        jnp.einsum("rhd,rchd->rhc", query_rows, key_rows, preferred_element_type=jnp.float32)
        * score_scale
        + bias_rows
    )
    positions = seq_index * ctx_local + jnp.arange(ctx_local, dtype=jnp.int32)
    valid_mask = (positions[None, :] < lengths[:, None])[:, None, :]
    cache_scores = jnp.where(valid_mask, cache_scores, -1e30)
    local_max = jnp.max(cache_scores, axis=-1)
    local_weights = jnp.where(valid_mask, jnp.exp(cache_scores - local_max[..., None]), 0.0)
    local_sum = jnp.sum(local_weights, axis=-1)
    local_acc = jnp.einsum(
        "rhc,rchd->rhd", local_weights, value_rows, precision=lax.Precision.HIGHEST
    )
    part_max, part_sum, part_acc = combined_all(
        (local_max, local_sum, local_acc), "seq", combine_parts
    )
    own_key = keys_new.reshape(request_count, heads_here, HD).astype(jnp.float32)
    own_value = values_new.reshape(request_count, heads_here, HD).astype(jnp.float32)
    own_score = (
        jnp.sum(query_rows.astype(jnp.float32) * own_key, axis=-1) * score_scale
        + bias_here[0][None, :]
    )
    row_peak = jnp.maximum(part_max, own_score)
    keep_scale = jnp.exp(part_max - row_peak)
    own_weight = jnp.exp(own_score - row_peak)
    weight_total = part_sum * keep_scale + own_weight
    weighted = part_acc * keep_scale[..., None] + own_weight[..., None] * own_value
    mixed_rows = (
        (weighted / weight_total[..., None])
        .astype(jnp.bfloat16)
        .reshape(request_count, heads_width)
    )
    head_terms = jnp.dot(mixed_rows, out_proj, preferred_element_type=jnp.float32)
    attended = lax.psum(head_terms, "tp")
    decode_hidden = (decode_in.astype(jnp.float32) + attended).astype(jnp.bfloat16)
    normed_dec = rms_scale(decode_hidden, norm_gain)
    my_expert = seq_index // shards
    dec_part = expert_block(normed_dec, weights).astype(jnp.float32)
    gate_here = jnp.sum(jnp.where(dec_routes == my_expert, dec_gates, 0.0), axis=1)
    dec_terms = lax.psum(gate_here[:, None] * dec_part, "seq")
    decode_out = (decode_hidden.astype(jnp.float32) + dec_terms).astype(jnp.bfloat16)
    send_all, index_all = pack_rows(normed_pre, routes, CAP, shards)
    back_all = lax.all_to_all(
        expert_apply(
            lax.all_to_all(send_all, "seq", split_axis=0, concat_axis=0, tiled=True), weights
        ),
        "seq",
        split_axis=0,
        concat_axis=0,
        tiled=True,
    )
    prefill_out = unpack_rows(back_all, index_all, shards, prefill_in, gates)
    return (decode_out, prefill_out)


def solution(mesh):
    placed = (
        P(None, "tp"),
        P(None, "tp"),
        P(None, "tp"),
        P(None, "seq", "tp"),
        P(None, "seq", "tp"),
        P(None, "seq"),
        P(),
        P(),
        P("tp", None),
        P(),
        P(("seq", "tp"), None),
        P(("seq", "tp"), None),
        P(("seq", "tp"), None),
        P(),
        P(),
        P(),
        P("tp", "seq"),
        P("tp", "seq"),
        P("seq", "tp"),
    )
    return jax.shard_map(
        body, mesh=mesh, in_specs=placed, out_specs=(P(), P(("seq", "tp"), None)), check_vma=False
    )
```

profile of v0, /device:TPU:8, one launch (start us, length us, event | category | flops | bytes accessed | tf_op | source)
XLA Modules:
  0.0 734.8 jit_solution(8691198079200414398)
XLA Ops:
  7.9 0.8 copy.57
  8.8 0.7 broadcast_multiply_fusion
  9.7 1.0 fusion.17
  10.8 1.0 fusion.19
  13.1 1.2 scatter_custom_fusion
  14.5 1.6 broadcast_in_dim.67
  16.1 18.7 %all-to-all-start = ((bf16[64,10,1024]{2,1,0:T(8,128)(2,1)}), bf16[64,10,1024]{2,1,0:T(8,128)(2,1)S(1)}, u32[]{:S(2)}, u32[]{:S(2)}) async-start(bf16[64,10,1024]{2,1,0:T(8,128)(2,1)} %bitcast.19), calls=%async_computation | async-start | bytes 4194304 | tf_op jit(solution)/shard_map/all_to_all | solution.py:168
  34.9 0.7 all-gather.11.cloned.1.call-update
  36.7 0.7 constant_dynamic-slice_fusion.1
  38.2 162.8 %all-gather.2 = f32[256,2,64]{2,1,0:T(2,128)S(1)} all-gather(f32[4,2,64]{2,1,0:T(2,128)S(1)} %bitcast.70), channel_id=4, replica_groups=mesh['seq'=64,'tp'=8] {'seq'}, dimensions={0}, use_global_device_ids=true | all-gather | bytes 133120 | tf_op jit(solution)/shard_map/all_gather | solution.py:14
  201.2 80.8 %all-gather.4 = f32[64,4,2]{1,2,0:T(2,128)S(1)} all-gather(f32[1,4,2]{1,2,0:T(2,128)S(1)} %bitcast.72), channel_id=3, replica_groups=mesh['seq'=64,'tp'=8] {'seq'}, dimensions={0}, use_global_device_ids=true | all-gather | bytes 2080 | tf_op jit(solution)/shard_map/all_gather | solution.py:14
  282.0 88.0 %all-gather.3 = f32[64,4,2]{1,2,0:T(2,128)S(1)} all-gather(f32[1,4,2]{1,2,0:T(2,128)S(1)} %bitcast.71), channel_id=2, replica_groups=mesh['seq'=64,'tp'=8] {'seq'}, dimensions={0}, use_global_device_ids=true | all-gather | bytes 2080 | tf_op jit(solution)/shard_map/all_gather | solution.py:14
  370.0 1.3 reshape.153
  371.3 4.4 fusion.68
  375.8 6.6 convolution_convert_fusion
  382.4 1.6 reshape.154
  384.1 14.8 %all-to-all-start.1 = ((bf16[64,10,1024]{2,1,0:T(8,128)(2,1)}), bf16[64,10,1024]{2,1,0:T(8,128)(2,1)S(1)}, u32[]{:S(2)}, u32[]{:S(2)}) async-start(bf16[64,10,1024]{2,1,0:T(8,128)(2,1)} %reshape.154), calls=%async_computation.1 | async-start | bytes 4194304 | tf_op jit(solution)/shard_map/all_to_all | solution.py:166
  399.0 18.6 %while.14 = (s32[]{:T(128)}, f32[4,2]{0,1:T(2,128)S(1)}, f32[4,2]{0,1:T(2,128)S(1)}, f32[4,2,64]{2,1,0:T(2,128)S(1)}, f32[63,4,2]{1,2,0:T(2,128)S(1)}, /*index=5...) while((s32[]{:T(128)}, f32[4,2]{0,1:T(2,128)S(1)}, f32[4,2]{0,1:T(2,128)S(1)}, ...), condition=%wide.region_3.4_spmd, body=%wide.region_2.3_spmd.sunk | while | flops 1586 | bytes 6685 | solution.py:17
  419.0 21.6 %psum.14 = f32[4,1024]{1,0:T(4,128)S(1)} all-reduce(f32[4,1024]{1,0:T(4,128)S(1)} %fusion.67), channel_id=1, replica_groups=mesh['seq'=64,'tp'=8] {'tp'}, use_global_device_ids=true, to_apply=%region_5.6 | all-reduce | flops 4096 | bytes 32768 | tf_op jit(solution)/shard_map/psum | solution.py:157
  440.8 1.8 fusion.59
  442.6 2.7 fusion.13
  445.3 279.1 %psum.15 = f32[4,1024]{1,0:T(4,128)S(1)} all-reduce(f32[4,1024]{1,0:T(4,128)S(1)} %fusion.13), channel_id=1, replica_groups=mesh['seq'=64,'tp'=8] {'seq'}, use_global_device_ids=true, to_apply=%region_8.9 | all-reduce | flops 4096 | bytes 32768 | tf_op jit(solution)/shard_map/psum | solution.py:163
  725.6 0.8 gather_fusion
  726.7 0.8 multiply_reduce_fusion
  (360 shorter events, 26.7 us)
Async XLA Ops:
  7.2 411.7 %copy-start = (bf16[128,1024]{1,0:T(8,128)(2,1)S(1)}, bf16[128,1024]{1,0:T(8,128)(2,1)}, u32[]{:S(2)}) copy-start(bf16[128,1024]{1,0:T(8,128)(2,1)} %param.29) | copy-start | bytes 786436
  7.2 364.1 %all-gather.9.cloned.1.call-start = ((), (), s32[]{:S(2)}) async-start(), calls=%async_computation.2 | async-start | bytes 1622016 | tf_op jit(solution)/shard_map/all_gather | solution.py:106
  16.1 20.2 %copy-start.6 = (bf16[4,64,128]{2,1,0:T(8,128)(2,1)S(1)}, bf16[4,64,128]{2,1,0:T(8,128)(2,1)}, u32[]{:S(2)}) copy-start(bf16[4,64,128]{2,1,0:T(8,128)(2,1)} %param.24) | copy-start | bytes 196612
  16.1 20.4 %copy-start.11 = (bf16[4,128]{1,0:T(4,128)(2,1)S(1)}, bf16[4,128]{1,0:T(4,128)(2,1)}, u32[]{:S(2)}) copy-start(bf16[4,128]{1,0:T(4,128)(2,1)} %param.21) | copy-start | bytes 3076
  16.1 20.5 %copy-start.7 = (bf16[4,64,128]{2,1,0:T(8,128)(2,1)S(1)}, bf16[4,64,128]{2,1,0:T(8,128)(2,1)}, u32[]{:S(2)}) copy-start(bf16[4,64,128]{2,1,0:T(8,128)(2,1)} %param.25) | copy-start | bytes 196612
  16.1 21.3 %copy-start.20 = (s32[4]{0:T(128)S(1)}, s32[4]{0:T(128)}, u32[]{:S(2)}) copy-start(s32[4]{0:T(128)} %param.27) | copy-start | bytes 52
  16.1 21.5 %copy-start.19 = (s32[4,64]{1,0:T(4,128)S(1)}, s32[4,64]{1,0:T(4,128)}, u32[]{:S(2)}) copy-start(s32[4,64]{1,0:T(4,128)} %param.26) | copy-start | bytes 3076
  16.1 353.8 %all-to-all-start = ((bf16[64,10,1024]{2,1,0:T(8,128)(2,1)}), bf16[64,10,1024]{2,1,0:T(8,128)(2,1)S(1)}, u32[]{:S(2)}, u32[]{:S(2)}) async-start(bf16[64,10,1024]{2,1,0:T(8,128)(2,1)} %bitcast.19), calls=%async_computation | async-start | bytes 4194304 | tf_op jit(solution)/shard_map/all_to_all | solution.py:168
  34.8 340.9 %all-gather.11.cloned.1.call-start = ((), (), s32[]{:S(2)}) async-start(), calls=%async_computation.3 | async-start | bytes 1622016 | tf_op jit(solution)/shard_map/all_gather | solution.py:107
  35.6 340.2 %all-gather.13.cloned.1.call-start = ((), (), s32[]{:S(2)}) async-start(), calls=%async_computation.4 | async-start | bytes 1622016 | tf_op jit(solution)/shard_map/all_gather | solution.py:108
  201.0 174.8 %copy-start.3 = (f32[256,2,64]{2,1,0:T(2,128)}, f32[256,2,64]{2,1,0:T(2,128)S(1)}, u32[]{:S(2)}) copy-start(f32[256,2,64]{2,1,0:T(2,128)S(1)} %all-gather.2) | copy-start | bytes 393220
  282.0 89.3 %copy-start.4 = (f32[64,4,2]{1,2,0:T(2,128)}, f32[64,4,2]{1,2,0:T(2,128)S(1)}, u32[]{:S(2)}) copy-start(f32[64,4,2]{1,2,0:T(2,128)S(1)} %all-gather.4) | copy-start | bytes 6148
  384.0 15.0 %slice-start.1 = ((f32[64,4,2]{1,2,0:T(2,128)}), f32[63,4,2]{1,2,0:T(2,128)S(1)}, s32[]{:S(2)}) async-start(f32[64,4,2]{1,2,0:T(2,128)} %copy-done.4), calls=%async_computation.6 | async-start | bytes 129024 | tf_op jit(solution)/shard_map/slice | solution.py:16
  384.0 15.0 %slice-start.2 = ((f32[64,4,2]{1,2,0:T(2,128)}), f32[63,4,2]{1,2,0:T(2,128)S(1)}, s32[]{:S(2)}) async-start(f32[64,4,2]{1,2,0:T(2,128)} %copy-done.5), calls=%async_computation.7 | async-start | bytes 129024 | tf_op jit(solution)/shard_map/slice | solution.py:16
  384.0 34.0 %copy-start.12 = (bf16[4,128]{1,0:T(4,128)(2,1)S(1)}, bf16[4,128]{1,0:T(4,128)(2,1)}, u32[]{:S(2)}) copy-start(bf16[4,128]{1,0:T(4,128)(2,1)} %param.22) | copy-start | bytes 3076
  384.0 34.0 %copy-start.13 = (bf16[4,128]{1,0:T(4,128)(2,1)S(1)}, bf16[4,128]{1,0:T(4,128)(2,1)}, u32[]{:S(2)}) copy-start(bf16[4,128]{1,0:T(4,128)(2,1)} %param.23) | copy-start | bytes 3076
  384.0 34.6 %copy-start.9 = (s32[64,2]{0,1:T(2,128)S(1)}, s32[64,2]{0,1:T(2,128)}, u32[]{:S(2)}) copy-start(s32[64,2]{0,1:T(2,128)} %param.32) | copy-start | bytes 1540
  384.0 34.7 %copy-start.14 = (f32[64,2]{0,1:T(2,128)S(1)}, f32[64,2]{0,1:T(2,128)}, u32[]{:S(2)}) copy-start(f32[64,2]{0,1:T(2,128)} %param.33) | copy-start | bytes 1540
  384.0 56.6 %copy-start.18 = (s32[128]{0:T(128)S(1)}, s32[128]{0:T(128)}, u32[]{:S(2)}) copy-start(s32[128]{0:T(128)} %copy-done.17) | copy-start | bytes 1540
  384.1 56.6 %copy-start.15 = (f32[4,2]{0,1:T(2,128)S(1)}, f32[4,2]{0,1:T(2,128)}, u32[]{:S(2)}) copy-start(f32[4,2]{0,1:T(2,128)} %param.35) | copy-start | bytes 100
  384.1 56.6 %copy-start.16 = (s32[4,2]{0,1:T(2,128)S(1)}, s32[4,2]{0,1:T(2,128)}, u32[]{:S(2)}) copy-start(s32[4,2]{0,1:T(2,128)} %param.34) | copy-start | bytes 100
  384.1 56.6 %copy-start.10 = (bf16[4,1024]{1,0:T(4,128)(2,1)S(1)}, bf16[4,1024]{1,0:T(4,128)(2,1)}, u32[]{:S(2)}) copy-start(bf16[4,1024]{1,0:T(4,128)(2,1)} %param.30) | copy-start | bytes 24580
  384.1 56.7 %copy-start.8 = (f32[1024]{0:T(1024)S(1)}, f32[1024]{0:T(1024)}, u32[]{:S(2)}) copy-start(f32[1024]{0:T(1024)} %param.36) | copy-start | bytes 12292
  384.1 341.0 %all-to-all-start.1 = ((bf16[64,10,1024]{2,1,0:T(8,128)(2,1)}), bf16[64,10,1024]{2,1,0:T(8,128)(2,1)S(1)}, u32[]{:S(2)}, u32[]{:S(2)}) async-start(bf16[64,10,1024]{2,1,0:T(8,128)(2,1)} %reshape.154), calls=%async_computation.1 | async-start | bytes 4194304 | tf_op jit(solution)/shard_map/all_to_all | solution.py:166
  (5 other events, 22.5 us)
Sparse Core Ops, SparseCore 0:
  10.1 36.1 all-gather.8
  48.5 33.4 all-gather.10
  84.0 33.4 all-gather.12
where the time goes:
time: 735 us
  blocking collectives  632 us (86%)
  starting transfers between devices  33.7 us (5%)
  local copies, waits for them, and re-layouts  23.1 us (3%)
  matrix products  16.3 us (2%)
  between operations  14.2 us (2%)
  other arithmetic  12.9 us (2%)
    all_gather x3, blocking collectives, combined_all(): pieces = jax.tree.map(lambda part: lax.all_gather(part, axis), value)  332 us
    psum x1, blocking collectives, body(): dec_terms = lax.psum(gate_here[:, None] * dec_part, 'seq')  279 us
    psum x1, blocking collectives, body(): attended = lax.psum(head_terms, 'tp')  21.6 us
    all_to_all x1, starting transfers between devices, body(): lax.all_to_all(send_all, 'seq', split_axis=0, concat_axis=0, tiled=True)  18.7 us
    all_to_all x1, starting transfers between devices, body(): lax.all_to_all(expert_apply(lax.all_to_all(send_all, 'seq', split_axis=0,...  14.8 us
  transfers between devices with their start and end apart: 5, of which 0 were waited for; matrix products, arithmetic and copies ran while one was open for 5% of the time, Pallas kernels for 0%

commit v1 on v0

--- a/solution.py
+++ b/solution.py
@@ -160,7 +160,8 @@
     my_expert = seq_index // shards
     dec_part = expert_block(normed_dec, weights).astype(jnp.float32)
     gate_here = jnp.sum(jnp.where(dec_routes == my_expert, dec_gates, 0.0), axis=1)
-    dec_terms = lax.psum(gate_here[:, None] * dec_part, "seq")
+    local_x = gate_here[:, None] * dec_part
+    dec_terms = jax.lax.all_gather(local_x, "seq").sum(axis=0)
     decode_out = (decode_hidden.astype(jnp.float32) + dec_terms).astype(jnp.bfloat16)
     send_all, index_all = pack_rows(normed_pre, routes, CAP, shards)
     back_all = lax.all_to_all(

time: 735 us -> 599 us (0.81)
  blocking collectives: 632 us -> 353 us
  waiting for transfers between devices: 2.08 us -> 142 us
    psum x1 -> x0, blocking collectives: 279 us -> none  [body(): dec_terms = lax.psum(gate_here[:, None] * dec_part, 'seq')]
    all_gather x0 -> x1, waiting for transfers between devices: none -> 140 us  [body(): dec_terms = jax.lax.all_gather(local_x, 'seq').sum(axis=0)]
  transfers between devices with their start and end apart: 5 -> 6, of which waited for: 0 -> 1; matrix products, arithmetic and copies ran while one was open for 5% -> 7% of each run, Pallas kernels for 0% -> 0%
where the time goes in v1:
time: 599 us; the launch traced here: 598 us
  blocking collectives  353 us (59%)
  waiting for transfers between devices  142 us (24%)
  starting transfers between devices  34 us (6%)
  local copies, waits for them, and re-layouts  22.9 us (4%)
  matrix products  16.9 us (3%)
  other arithmetic  14.3 us (2%)
  between operations  14.2 us (2%)
    all_gather x3, blocking collectives, combined_all(): pieces = jax.tree.map(lambda part: lax.all_gather(part, axis), value)  331 us
    all_gather x1, waiting for transfers between devices, body(): dec_terms = jax.lax.all_gather(local_x, 'seq').sum(axis=0)  140 us
    psum x1, blocking collectives, body(): attended = lax.psum(head_terms, 'tp')  21.6 us
    all_to_all x1, starting transfers between devices, body(): lax.all_to_all(send_all, 'seq', split_axis=0, concat_axis=0, tiled=True)  18.7 us
    all_to_all x1, starting transfers between devices, body(): lax.all_to_all(expert_apply(lax.all_to_all(send_all, 'seq', split_axis=0,...  15.2 us
  transfers between devices with their start and end apart: 6, of which 1 were waited for; matrix products, arithmetic and copies ran while one was open for 7% of the time, Pallas kernels for 0%

profile of v1, /device:TPU:8, one launch (start us, length us, event | category | flops | bytes accessed | tf_op | source)
XLA Modules:
  0.0 598.0 jit_solution(11617097017761749064)
XLA Ops:
  7.9 0.8 copy.57
  9.7 1.0 fusion.18
  10.8 1.0 fusion.20
  13.0 1.2 scatter_custom_fusion
  14.4 1.6 broadcast_in_dim.67
  16.0 18.7 %all-to-all-start = ((bf16[64,10,1024]{2,1,0:T(8,128)(2,1)}), bf16[64,10,1024]{2,1,0:T(8,128)(2,1)S(1)}, u32[]{:S(2)}, u32[]{:S(2)}) async-start(bf16[64,10,1024]{2,1,0:T(8,128)(2,1)} %bitcast.20), calls=%async_computation | async-start | bytes 4194304 | tf_op jit(solution)/shard_map/all_to_all | solution.py:169
  34.8 0.7 all-gather.14.cloned.1.call-update
  36.6 0.7 constant_dynamic-slice_fusion.1
  38.1 162.8 %all-gather.2 = f32[256,2,64]{2,1,0:T(2,128)S(1)} all-gather(f32[4,2,64]{2,1,0:T(2,128)S(1)} %bitcast.72), channel_id=4, replica_groups=mesh['seq'=64,'tp'=8] {'seq'}, dimensions={0}, use_global_device_ids=true | all-gather | bytes 133120 | tf_op jit(solution)/shard_map/all_gather | solution.py:14
  201.1 80.8 %all-gather.5 = f32[64,4,2]{1,2,0:T(2,128)S(1)} all-gather(f32[1,4,2]{1,2,0:T(2,128)S(1)} %bitcast.74), channel_id=3, replica_groups=mesh['seq'=64,'tp'=8] {'seq'}, dimensions={0}, use_global_device_ids=true | all-gather | bytes 2080 | tf_op jit(solution)/shard_map/all_gather | solution.py:14
  281.9 87.9 %all-gather.4 = f32[64,4,2]{1,2,0:T(2,128)S(1)} all-gather(f32[1,4,2]{1,2,0:T(2,128)S(1)} %bitcast.73), channel_id=2, replica_groups=mesh['seq'=64,'tp'=8] {'seq'}, dimensions={0}, use_global_device_ids=true | all-gather | bytes 2080 | tf_op jit(solution)/shard_map/all_gather | solution.py:14
  369.7 1.3 reshape.153
  371.1 4.4 fusion.69
  375.5 6.6 %convolution_convert_fusion = bf16[640,1024]{1,0:T(8,128)(2,1)S(1)} fusion(bf16[704,1024]{1,0:T(8,128)(2,1)} %all-gather.16.cloned.1.call-done, f32[640,704]{0,1:T(8,128)} %fusion.69, bf16[640,1024]{1,0:T(8,128)(2,1)S(1)} %copy-done.1, bf16[1024,704]{0,1:T(8,128)(2,1)} %all-gather.14.cloned.1.call-done), kind=kOutput, calls=%fused_computation.22 | convolution fusion | flops 1850654720 | bytes 7307264 | tf_op jit(solution)/shard_map/dot_general | solution.py:62
  382.1 1.6 reshape.154
  383.8 15.2 %all-to-all-start.1 = ((bf16[64,10,1024]{2,1,0:T(8,128)(2,1)}), bf16[64,10,1024]{2,1,0:T(8,128)(2,1)S(1)}, u32[]{:S(2)}, u32[]{:S(2)}) async-start(bf16[64,10,1024]{2,1,0:T(8,128)(2,1)} %reshape.154), calls=%async_computation.1 | async-start | bytes 4194304 | tf_op jit(solution)/shard_map/all_to_all | solution.py:167
  399.0 18.6 %while.14 = (s32[]{:T(128)}, f32[4,2]{0,1:T(2,128)S(1)}, f32[4,2]{0,1:T(2,128)S(1)}, f32[4,2,64]{2,1,0:T(2,128)S(1)}, f32[63,4,2]{1,2,0:T(2,128)S(1)}, /*index=5...) while((s32[]{:T(128)}, f32[4,2]{0,1:T(2,128)S(1)}, f32[4,2]{0,1:T(2,128)S(1)}, ...), condition=%wide.region_3.4_spmd, body=%wide.region_2.3_spmd.sunk | while | flops 1586 | bytes 6685 | solution.py:17
  418.6 21.6 %psum.7 = f32[4,1024]{1,0:T(4,128)S(1)} all-reduce(f32[4,1024]{1,0:T(4,128)S(1)} %fusion.68), channel_id=1, replica_groups=mesh['seq'=64,'tp'=8] {'tp'}, use_global_device_ids=true, to_apply=%region_5.6 | all-reduce | flops 4096 | bytes 32768 | tf_op jit(solution)/shard_map/psum | solution.py:157
  440.4 1.8 fusion.60
  442.2 3.3 fusion.14
  446.1 140.3 %all-gather.18.cloned.1.call-done = f32[64,4,1024]{2,1,0:T(4,128)} async-done(((f32[1,4,1024]{2,1,0:T(4,128)}), f32[64,4,1024]{2,1,0:T(4,128)}) %all-gather.18.cloned.1.call-update) | async-done | bytes 1048592 | tf_op jit(solution)/shard_map/all_gather | solution.py:164
  586.3 1.4 reduce_sum.89
  588.9 0.8 gather_fusion
  590.0 0.8 multiply_reduce_fusion
  (363 shorter events, 27.3 us)
Async XLA Ops:
  7.2 411.3 %copy-start = (bf16[128,1024]{1,0:T(8,128)(2,1)S(1)}, bf16[128,1024]{1,0:T(8,128)(2,1)}, u32[]{:S(2)}) copy-start(bf16[128,1024]{1,0:T(8,128)(2,1)} %param.29) | copy-start | bytes 786436
  7.2 363.9 %all-gather.12.cloned.1.call-start = ((), (), s32[]{:S(2)}) async-start(), calls=%async_computation.2 | async-start | bytes 1622016 | tf_op jit(solution)/shard_map/all_gather | solution.py:106
  16.0 20.2 %copy-start.6 = (bf16[4,64,128]{2,1,0:T(8,128)(2,1)S(1)}, bf16[4,64,128]{2,1,0:T(8,128)(2,1)}, u32[]{:S(2)}) copy-start(bf16[4,64,128]{2,1,0:T(8,128)(2,1)} %param.24) | copy-start | bytes 196612
  16.0 20.4 %copy-start.11 = (bf16[4,128]{1,0:T(4,128)(2,1)S(1)}, bf16[4,128]{1,0:T(4,128)(2,1)}, u32[]{:S(2)}) copy-start(bf16[4,128]{1,0:T(4,128)(2,1)} %param.21) | copy-start | bytes 3076
  16.0 20.5 %copy-start.7 = (bf16[4,64,128]{2,1,0:T(8,128)(2,1)S(1)}, bf16[4,64,128]{2,1,0:T(8,128)(2,1)}, u32[]{:S(2)}) copy-start(bf16[4,64,128]{2,1,0:T(8,128)(2,1)} %param.25) | copy-start | bytes 196612
  16.0 21.3 %copy-start.20 = (s32[4]{0:T(128)S(1)}, s32[4]{0:T(128)}, u32[]{:S(2)}) copy-start(s32[4]{0:T(128)} %param.27) | copy-start | bytes 52
  16.0 21.5 %copy-start.19 = (s32[4,64]{1,0:T(4,128)S(1)}, s32[4,64]{1,0:T(4,128)}, u32[]{:S(2)}) copy-start(s32[4,64]{1,0:T(4,128)} %param.26) | copy-start | bytes 3076
  16.0 353.7 %all-to-all-start = ((bf16[64,10,1024]{2,1,0:T(8,128)(2,1)}), bf16[64,10,1024]{2,1,0:T(8,128)(2,1)S(1)}, u32[]{:S(2)}, u32[]{:S(2)}) async-start(bf16[64,10,1024]{2,1,0:T(8,128)(2,1)} %bitcast.20), calls=%async_computation | async-start | bytes 4194304 | tf_op jit(solution)/shard_map/all_to_all | solution.py:169
  34.7 340.8 %all-gather.14.cloned.1.call-start = ((), (), s32[]{:S(2)}) async-start(), calls=%async_computation.3 | async-start | bytes 1622016 | tf_op jit(solution)/shard_map/all_gather | solution.py:107
  35.5 340.1 %all-gather.16.cloned.1.call-start = ((), (), s32[]{:S(2)}) async-start(), calls=%async_computation.4 | async-start | bytes 1622016 | tf_op jit(solution)/shard_map/all_gather | solution.py:108
  200.9 174.7 %copy-start.3 = (f32[256,2,64]{2,1,0:T(2,128)}, f32[256,2,64]{2,1,0:T(2,128)S(1)}, u32[]{:S(2)}) copy-start(f32[256,2,64]{2,1,0:T(2,128)S(1)} %all-gather.2) | copy-start | bytes 393220
  281.9 89.2 %copy-start.4 = (f32[64,4,2]{1,2,0:T(2,128)}, f32[64,4,2]{1,2,0:T(2,128)S(1)}, u32[]{:S(2)}) copy-start(f32[64,4,2]{1,2,0:T(2,128)S(1)} %all-gather.5) | copy-start | bytes 6148
  371.1 4.4 copy-start.1
  383.7 15.3 %slice-start = ((f32[256,2,64]{2,1,0:T(2,128)}), f32[4,2,64]{2,1,0:T(2,128)S(1)}, s32[]{:S(2)}) async-start(f32[256,2,64]{2,1,0:T(2,128)} %copy-done.3), calls=%async_computation.6 | async-start | bytes 8192 | tf_op jit(solution)/shard_map/slice | solution.py:15
  383.7 15.3 %slice-start.1 = ((f32[64,4,2]{1,2,0:T(2,128)}), f32[63,4,2]{1,2,0:T(2,128)S(1)}, s32[]{:S(2)}) async-start(f32[64,4,2]{1,2,0:T(2,128)} %copy-done.4), calls=%async_computation.7 | async-start | bytes 129024 | tf_op jit(solution)/shard_map/slice | solution.py:16
  383.7 15.3 %slice-start.2 = ((f32[64,4,2]{1,2,0:T(2,128)}), f32[63,4,2]{1,2,0:T(2,128)S(1)}, s32[]{:S(2)}) async-start(f32[64,4,2]{1,2,0:T(2,128)} %copy-done.5), calls=%async_computation.8 | async-start | bytes 129024 | tf_op jit(solution)/shard_map/slice | solution.py:16
  383.7 34.2 %copy-start.12 = (bf16[4,128]{1,0:T(4,128)(2,1)S(1)}, bf16[4,128]{1,0:T(4,128)(2,1)}, u32[]{:S(2)}) copy-start(bf16[4,128]{1,0:T(4,128)(2,1)} %param.22) | copy-start | bytes 3076
  383.7 34.2 %copy-start.13 = (bf16[4,128]{1,0:T(4,128)(2,1)S(1)}, bf16[4,128]{1,0:T(4,128)(2,1)}, u32[]{:S(2)}) copy-start(bf16[4,128]{1,0:T(4,128)(2,1)} %param.23) | copy-start | bytes 3076
  383.7 56.5 %copy-start.14 = (f32[4,2]{0,1:T(2,128)S(1)}, f32[4,2]{0,1:T(2,128)}, u32[]{:S(2)}) copy-start(f32[4,2]{0,1:T(2,128)} %param.35) | copy-start | bytes 100
  383.7 56.5 %copy-start.15 = (s32[4,2]{0,1:T(2,128)S(1)}, s32[4,2]{0,1:T(2,128)}, u32[]{:S(2)}) copy-start(s32[4,2]{0,1:T(2,128)} %param.34) | copy-start | bytes 100
  383.7 56.5 %copy-start.10 = (bf16[4,1024]{1,0:T(4,128)(2,1)S(1)}, bf16[4,1024]{1,0:T(4,128)(2,1)}, u32[]{:S(2)}) copy-start(bf16[4,1024]{1,0:T(4,128)(2,1)} %param.30) | copy-start | bytes 24580
  383.8 56.6 %copy-start.8 = (f32[1024]{0:T(1024)S(1)}, f32[1024]{0:T(1024)}, u32[]{:S(2)}) copy-start(f32[1024]{0:T(1024)} %param.36) | copy-start | bytes 12292
  383.8 204.6 %all-to-all-start.1 = ((bf16[64,10,1024]{2,1,0:T(8,128)(2,1)}), bf16[64,10,1024]{2,1,0:T(8,128)(2,1)S(1)}, u32[]{:S(2)}, u32[]{:S(2)}) async-start(bf16[64,10,1024]{2,1,0:T(8,128)(2,1)} %reshape.154), calls=%async_computation.1 | async-start | bytes 4194304 | tf_op jit(solution)/shard_map/all_to_all | solution.py:167
  398.9 187.4 %all-gather.18.cloned.1.call-start = ((), (), s32[]{:S(2)}) async-start(), calls=%async_computation.5 | async-start | bytes 1064960 | tf_op jit(solution)/shard_map/all_gather | solution.py:164
  (6 other events, 14.2 us)
Sparse Core Ops, SparseCore 0:
  10.1 36.1 all-gather.11
  48.5 33.4 all-gather.13
  84.0 33.4 all-gather.15
  445.7 140.5 all-gather.17
